TPU v7x, 32 devices: a whole 2x2x4 slice. The times are simulated.
32 devices in a mesh: grp: 2 (over y), gen: 4 (over z), row: 2 (over x), ch: 2 (over core).
Axes of the slice: x: 2, y: 2, z: 4, core: 2. Of those that a mesh axis runs over, the one named last changes fastest.
Arguments:
- x_center: bfloat16 [24, 24, 112], P(('grp', 'row')), parts along dimension 0, may hold values from -6 to 6
- x_gens: bfloat16 [256, 12, 24, 112], P(('grp', 'gen'), 'row'), parts along dimension 0, may hold values from -0.125 to 0.125
- w_expand: bfloat16 [112, 672], P(None, 'ch'), may hold values from -0.5 to 0.5
- b_expand: float32 [672], P('ch'), may hold values from -3 to 3
- w_depth: float32 [5, 5, 672], P(None, None, 'ch'), may hold values from -1.25 to 1.25
- b_depth: float32 [672], P('ch'), may hold values from -3 to 3
- w_reduce: float32 [672, 28], replicated, may hold values from -0.25 to 0.25
- b_reduce: float32 [28], replicated, may hold values from -6 to 6
- w_excite: float32 [28, 672], P(None, 'ch'), may hold values from -1 to 1
- b_excite: float32 [672], P('ch'), may hold values from -3 to 3
Outputs:
- out_center: float32 [24, 24, 672], P(('grp', 'row'), None, 'ch'), parts along dimension 0
- out_gens: bfloat16 [256, 12, 24, 672], P(('grp', 'gen'), 'row', None, 'ch'), parts along dimension 0
- out_box: float32 [24, 24, 672], P(('grp', 'row'), None, 'ch'), parts along dimension 0
There are 2 independent parts, one for each index of `grp`. A program takes and returns all parts, laid end to end along the dimension named above; an argument that names none is the same for every part. Nothing has to cross between parts.
All inputs are finite; a program needn't handle non-finite values.
Results may differ from a plain program's by a relative error of at most 0.007.
Values may be sent and summed in bfloat16 or wider, within the bound.
A program may use at most 64 MiB of HBM per device.

v0:
```python
import jax
import jax.numpy as jnp
from jax import lax
from jax.sharding import PartitionSpec as P


def padded_2(cells, sides, width):
    for axis, dim in sides:
        count = lax.axis_size(axis)
        ends = count - 1
        head = lax.slice_in_dim(cells, 0, width, axis=dim)
        tail = lax.slice_in_dim(cells, cells.shape[dim] - width, cells.shape[dim], axis=dim)
        cells = jnp.concatenate(
            [
                lax.ppermute(tail, axis, [(i, (i + 1) % count) for i in range(ends)]),
                cells,
                lax.ppermute(head, axis, [((i + 1) % count, i) for i in range(ends)]),
            ],
            axis=dim,
        )
    return cells


def depthwise(padded, w_depth, row_count, col_count):
    accum_sum = jnp.zeros(padded.shape[:-3] + (row_count, col_count, padded.shape[-1]), jnp.float32)
    for tap_row in range(w_depth.shape[0]):
        for tap_col in range(w_depth.shape[1]):
            window = padded[..., tap_row : tap_row + row_count, tap_col : tap_col + col_count, :]
            accum_sum = accum_sum + window.astype(jnp.float32) * w_depth[tap_row, tap_col]
    return accum_sum


def relax_gate(ex_center, gate_radius):
    low_end = ex_center - gate_radius
    high_end = ex_center + gate_radius
    sig_low = jax.nn.sigmoid(low_end)
    sig_high = jax.nn.sigmoid(high_end)
    slope_val = jnp.minimum(sig_low * (1.0 - sig_low), sig_high * (1.0 - sig_high))
    gate_center = slope_val * ex_center + 0.5 * (
        sig_high + sig_low - slope_val * (high_end + low_end)
    )
    spread_term = 0.5 * (sig_high - sig_low - slope_val * (high_end - low_end))
    return (gate_center, slope_val, spread_term)


def on_device(
    x_center, x_gens, w_expand, b_expand, w_depth, b_depth, w_reduce, b_reduce, w_excite, b_excite
):
    precise = lax.Precision.HIGHEST
    row_count = x_center.shape[0]
    col_count = x_center.shape[1]
    margin = w_depth.shape[0] // 2
    height = row_count * lax.axis_size("row")
    own_center = (
        jnp.dot(x_center, w_expand, preferred_element_type=jnp.float32) + b_expand
    ).astype(jnp.bfloat16)
    own_gens = jnp.dot(x_gens, w_expand, preferred_element_type=jnp.float32).astype(jnp.bfloat16)
    padded_center, exp_gens = (
        padded_2(own_center[None], (("row", 1),), margin),
        padded_2(own_gens, (("row", 1),), margin),
    )
    exp_center = padded_center[0]
    dw_center = (
        depthwise(
            jnp.pad(exp_center, ((0, 0), (margin, margin), (0, 0))), w_depth, row_count, col_count
        )
        + b_depth
    )
    dw_gens = depthwise(
        jnp.pad(exp_gens, ((0, 0), (0, 0), (margin, margin), (0, 0))), w_depth, row_count, col_count
    ).astype(jnp.bfloat16)
    local_radius = jnp.sum(jnp.abs(dw_gens).astype(jnp.float32), axis=0)
    feat_radius = lax.psum(local_radius.astype(jnp.bfloat16), "gen").astype(jnp.float32)
    inv_cells = 1.0 / (height * col_count)
    pool_center = jnp.sum(dw_center, axis=(0, 1)) * inv_cells
    pool_gens = jnp.sum(dw_gens.astype(jnp.float32), axis=(1, 2)) * inv_cells
    pool_center, pool_gens = lax.psum((pool_center, pool_gens), "row")
    pool_center, pool_gens = (
        lax.all_gather(pool_center, "ch", axis=0, tiled=True),
        lax.all_gather(pool_gens, "ch", axis=1, tiled=True),
    )
    sq_center = jnp.dot(pool_center, w_reduce, precision=precise) + b_reduce
    sq_gens = jnp.dot(pool_gens, w_reduce, precision=precise)
    ex_center = jnp.dot(sq_center, w_excite, precision=precise) + b_excite
    ex_gens = jnp.dot(sq_gens, w_excite, precision=precise)
    local_gate = jnp.sum(jnp.abs(ex_gens), axis=0)
    gate_radius = lax.psum(local_gate, "gen")
    gate_center, slope_val, spread_term = relax_gate(ex_center, gate_radius)
    gate_gens = slope_val * ex_gens
    gate_total = slope_val * gate_radius + spread_term
    out_center = dw_center * gate_center
    out_gens = (
        dw_center[None] * gate_gens[:, None, None, :] + gate_center * dw_gens.astype(jnp.float32)
    ).astype(jnp.bfloat16)
    out_box = jnp.abs(dw_center) * spread_term + feat_radius * gate_total
    return (out_center, out_gens, out_box)


def solution(mesh):
    in_specs = (
        P(("grp", "row"), None, None),
        P(("grp", "gen"), "row", None, None),
        P(None, "ch"),
        P("ch"),
        P(None, None, "ch"),
        P("ch"),
        P(),
        P(),
        P(None, "ch"),
        P("ch"),
    )
    out_specs = (
        P(("grp", "row"), None, "ch"),
        P(("grp", "gen"), "row", None, "ch"),
        P(("grp", "row"), None, "ch"),
    )
    return jax.shard_map(
        on_device, mesh=mesh, in_specs=in_specs, out_specs=out_specs, check_vma=False
    )
```

profile of v0, /device:TPU:0, one launch (start us, length us, event | category | flops | bytes accessed | tf_op | source)
XLA Modules:
  0.0 158.3 jit_solution(7868067441693738180)
XLA Ops:
  7.2 0.0 copy-start
  7.2 0.0 copy-start.30
  7.2 0.0 copy-start.7
  7.2 0.0 copy-start.8
  7.2 0.0 copy-start.28
  7.2 0.0 copy-start.9
  7.2 0.0 all-reduce.6.cloned.1.call-start
  7.3 1.3 copy-done
  8.5 2.3 %convolution_convert_fusion = bf16[32,6,24,336]{3,2,1,0:T(8,128)(2,1)S(1)} fusion(bf16[32,6,24,112]{3,2,1,0:T(8,128)(2,1)S(1)} %copy-done, bf16[112,336]{1,0:T(8,128)(2,1)} %param.12), kind=kOutput, calls=%fused_computation.22 | convolution fusion | flops 348364800 | bytes 4204032 | tf_op jit(solution)/shard_map/dot_general | solution.py:57
  10.8 0.0 copy-start.1
  10.8 1.8 %copy-done.1 = bf16[32,6,24,336]{3,2,1,0:T(8,128)(2,1)} copy-done((bf16[32,6,24,336]{3,2,1,0:T(8,128)(2,1)}, bf16[32,6,24,336]{3,2,1,0:T(8,128)(2,1)S(1)}, u32[]{:S(2)}) %copy-start.1) | copy-done | bytes 3096600
  12.6 1.6 %fusion.48 = (bf16[32,2,24,336]{3,2,1,0:T(8,128)(2,1)}, bf16[32,2,24,336]{3,2,1,0:T(8,128)(2,1)}) fusion(bf16[32,6,24,336]{3,2,1,0:T(8,128)(2,1)S(1)} %convolution_convert_fusion), kind=kLoop, calls=%fused_computation.132 | loop fusion | bytes 4128768 | tf_op jit(solution)/shard_map/slice | solution.py:12
  14.3 4.9 %collective-permute-start.2 = (bf16[32,2,24,336]{3,2,1,0:T(8,128)(2,1)}, bf16[32,2,24,336]{3,2,1,0:T(8,128)(2,1)S(1)}, u32[]{:S(2)}, u32[]{:S(2)}) collective-permute-start(bf16[32,2,24,336]{3,2,1,0:T(8,128)(2,1)} %get-tuple-element.36), channel_id=1, source_target_pairs={{0,2},{1,3},{4,6},{5,7},{8,10},{9,11},{12,14},{13,15},{16,18},{17,... | collective-permute-start | bytes 3096584 | tf_op jit(solution)/shard_map/ppermute | solution.py:15
  19.2 1.3 collective-permute-start.3
  20.5 0.2 fusion.10
  20.7 5.6 %collective-permute-start = (bf16[1,2,24,336]{3,2,1,0:T(8,128)(2,1)S(1)}, bf16[1,2,24,336]{3,2,1,0:T(8,128)(2,1)S(1)}, u32[]{:S(2)}, u32[]{:S(2)}) collective-permute-start(bf16[1,2,24,336]{3,2,1,0:T(8,128)(2,1)S(1)} %get-tuple-element.40), channel_id=1, source_target_pairs={{0,2},{1,3},{4,6},{5,7},{8,10},{9,11},{12,14},{13,15},{16,18},{17,... | collective-permute-start | bytes 96776 | tf_op jit(solution)/shard_map/ppermute | solution.py:15
  26.3 1.3 collective-permute-start.1
  27.6 0.1 slice_reduce_fusion.24
  27.9 0.6 dynamic-slice
  29.2 16.1 %collective-permute-done = bf16[1,2,24,336]{3,2,1,0:T(8,128)(2,1)S(1)} collective-permute-done((bf16[1,2,24,336]{3,2,1,0:T(8,128)(2,1)S(1)}, bf16[1,2,24,336]{3,2,1,0:T(8,128)(2,1)S(1)}, u32[]{:S(2)}, u32[]{:S(2)}) %collective-permute-start) | collective-permute-done | bytes 32288 | tf_op jit(solution)/shard_map/ppermute | solution.py:15
  45.3 4.2 %collective-permute-done.1 = bf16[1,2,24,336]{3,2,1,0:T(8,128)(2,1)S(1)} collective-permute-done((bf16[1,2,24,336]{3,2,1,0:T(8,128)(2,1)S(1)}, bf16[1,2,24,336]{3,2,1,0:T(8,128)(2,1)S(1)}, u32[]{:S(2)}, u32[]{:S(2)}) %collective-permute-start.1) | collective-permute-done | bytes 32288 | tf_op jit(solution)/shard_map/ppermute | solution.py:17
  49.5 0.0 copy-start.2
  49.6 1.3 fusion.46
  50.9 0.6 broadcast_multiply_fusion.3
  51.5 0.0 collective-permute-done.2
  51.7 1.0 copy-done.4
  52.7 0.0 collective-permute-done.3
  52.7 5.7 %fusion.5 = bf16[32,10,28,336]{3,2,1,0:T(8,128)(2,1)S(1)} fusion(bf16[32,2,24,336]{3,2,1,0:T(8,128)(2,1)} %collective-permute-done.3, bf16[32,6,24,336]{3,2,1,0:T(8,128)(2,1)} %copy-done.1, bf16[32,2,24,336]{3,2,1,0:T(8,128)(2,1)} %copy-done.4), kind=kLoop, calls=%fused_computation.9 | loop fusion | flops 36126720 | bytes 11182080 | tf_op jit(solution)/shard_map/concatenate | solution.py:13
  58.4 0.0 copy-start.6
  58.5 27.4 %abs_reduce_fusion = (bf16[6,24,336]{2,1,0:T(8,128)(2,1)}, bf16[32,6,24,336]{3,2,1,0:T(8,128)(2,1)S(1)}) fusion(f32[336]{0:T(512)} %copy-done.26, bf16[32,10,28,336]{3,2,1,0:T(8,128)(2,1)S(1)} %fusion.5, f32[336]{0:T(512)} %copy-done.27, f32[336]{0:T(512)S(1)} %get-tuple-element.4, bf16[32,2,24,336]{3,2,1,0:T(8,128)(2,1)} %collective-permute-done.3, ...), kind=kLoop, calls=%fused_computation.21 | loop fusion | flops 125362944 | bytes 70319424 | tf_op jit(solution)/shard_map/reduce_sum | solution.py:72
  85.9 1.8 %copy-done.3 = bf16[32,6,24,336]{3,2,1,0:T(8,128)(2,1)} copy-done((bf16[32,6,24,336]{3,2,1,0:T(8,128)(2,1)}, bf16[32,6,24,336]{3,2,1,0:T(8,128)(2,1)S(1)}, u32[]{:S(2)}) %copy-start.3) | copy-done | bytes 3096600
  87.7 0.6 convert_reduce_fusion
  88.3 7.8 %all-reduce.3 = (f32[336]{0:T(512)S(1)}, f32[32,336]{1,0:T(8,128)S(1)}) all-reduce(f32[336]{0:T(512)} %broadcast_multiply_fusion.3, f32[32,336]{1,0:T(8,128)S(1)} %broadcast_multiply_fusion.2), channel_id=1, replica_groups=mesh['grp'=2,'gen'=4,'row'=2,'ch'=2] {'row'}, use_global_device_ids=true, to_apply=%region_1.2 | all-reduce | flops 11088 | bytes 88704 | tf_op jit(solution)/shard_map/psum | solution.py:77
  96.1 1.9 %all-gather = f32[2,336,32]{1,2,0:T(8,128)S(1)} all-gather(f32[1,336,32]{1,2,0:T(8,128)S(1)} %bitcast.62), channel_id=1, replica_groups=mesh['grp'=2,'gen'=4,'row'=2,'ch'=2] {'ch'}, dimensions={0}, use_global_device_ids=true | all-gather | bytes 129024 | tf_op jit(solution)/shard_map/all_gather | solution.py:80
  98.0 0.1 copy.13
  98.1 0.1 reshape.62
  98.2 0.2 fusion.50
  98.4 1.0 abs_reduce_fusion.1
  99.4 12.0 %psum.30 = f32[336]{0:T(512)S(1)} all-reduce(f32[336]{0:T(512)S(1)} %get-tuple-element.45), channel_id=1, replica_groups=mesh['grp'=2,'gen'=4,'row'=2,'ch'=2] {'gen'}, use_global_device_ids=true, to_apply=%region_5.6 | all-reduce | flops 336 | bytes 2688 | tf_op jit(solution)/shard_map/psum | solution.py:87
  111.4 0.2 dynamic-update-slice
  111.6 2.4 %all-reduce.2 = f32[672]{0:T(1024)S(1)} all-reduce(f32[672]{0:T(1024)S(1)} %dynamic-update-slice), channel_id=1, replica_groups=mesh['grp'=2,'gen'=4,'row'=2,'ch'=2] {'ch'}, use_global_device_ids=true, to_apply=%add.2 | all-reduce | flops 672 | bytes 5376
  114.1 0.8 fusion.12
  114.9 1.0 convolution_reduce_fusion
  115.9 0.7 subtract_multiply_fusion.2
  116.6 0.0 all-reduce.6.cloned.1.call-update
  116.7 5.0 %fusion.7 = bf16[32,6,24,336]{3,2,1,0:T(8,128)(2,1)} fusion(bf16[32,6,24,336]{3,2,1,0:T(8,128)(2,1)} %copy-done.3, f32[336]{0:T(512)S(1)} %get-tuple-element.43, f32[32,336]{1,0:T(8,128)S(1)} %broadcast_multiply_fusion.1, f32[6,24,336]{2,1,0:T(8,128)} %get-tuple-element.35), kind=kLoop, calls=%fused_computation.11 | loop fusion | flops 7741440 | bytes 6431040 | tf_op jit(solution)/shard_map/convert_element_type | solution.py:94
  121.7 28.1 %all-reduce.6.cloned.1.call-done = bf16[6,24,336]{2,1,0:T(8,128)(2,1)} async-done(((bf16[6,24,336]{2,1,0:T(8,128)(2,1)}), bf16[6,24,336]{2,1,0:T(8,128)(2,1)}) %all-reduce.6.cloned.1.call-update) | async-done | bytes 96784 | tf_op jit(solution)/shard_map/psum | solution.py:73
  149.7 1.7 %multiply_add_fusion = (f32[6,24,336]{2,1,0:T(8,128)}, f32[6,24,336]{2,1,0:T(8,128)}) fusion(bf16[6,24,336]{2,1,0:T(8,128)(2,1)} %all-reduce.6.cloned.1.call-done, f32[6,24,336]{2,1,0:T(8,128)S(1)} %copy-done.5, f32[336]{0:T(512)S(1)} %get-tuple-element.42, f32[336]{0:T(512)S(1)} %get-tuple-element.30, f32[336]{0:T(512)S(1)} %get-tuple-element.43), kind=kLoop, calls=%fused_computation.77 | loop fusion | flops 290304 | bytes 681408 | tf_op jit(solution)/shard_map/add | solution.py:95
  (57 shorter events, 0.3 us)
Async XLA Ops:
  7.2 1.4 copy-start
  7.2 20.7 %copy-start.30 = (u32[32]{0:T(128)S(1)}, u32[32]{0:T(128)}, u32[]{:S(2)}) copy-start(u32[32]{0:T(128)} %constant.20) | copy-start | bytes 388
  7.2 13.3 %copy-start.7 = (bf16[112,336]{1,0:T(8,128)(2,1)S(1)}, bf16[112,336]{1,0:T(8,128)(2,1)}, u32[]{:S(2)}) copy-start(bf16[112,336]{1,0:T(8,128)(2,1)} %param.12) | copy-start | bytes 225796
  7.2 13.3 %copy-start.8 = (bf16[6,24,112]{2,1,0:T(8,128)(2,1)S(1)}, bf16[6,24,112]{2,1,0:T(8,128)(2,1)}, u32[]{:S(2)}) copy-start(bf16[6,24,112]{2,1,0:T(8,128)(2,1)} %param.10) | copy-start | bytes 96772
  7.2 13.3 %copy-start.28 = (f32[336]{0:T(512)S(1)}, f32[336]{0:T(512)}, u32[]{:S(2)}) copy-start(f32[336]{0:T(512)} %param.13) | copy-start | bytes 4036
  7.2 20.4 %copy-start.9 = (f32[5,5,336]{2,1,0:T(8,128)S(1)}, f32[5,5,336]{2,1,0:T(8,128)}, u32[]{:S(2)}) copy-start(f32[5,5,336]{2,1,0:T(8,128)} %param.14) | copy-start | bytes 100804
  7.2 42.3 %copy-start.29 = (f32[336]{0:T(512)S(1)}, f32[336]{0:T(512)}, u32[]{:S(2)}) copy-start(f32[336]{0:T(512)} %param.15) | copy-start | bytes 4036
  7.2 142.5 %all-reduce.6.cloned.1.call-start = ((), (), s32[]{:S(2)}) async-start(), calls=%async_computation | async-start | bytes 221184 | tf_op jit(solution)/shard_map/psum | solution.py:73
  10.8 1.8 %copy-start.1 = (bf16[32,6,24,336]{3,2,1,0:T(8,128)(2,1)}, bf16[32,6,24,336]{3,2,1,0:T(8,128)(2,1)S(1)}, u32[]{:S(2)}) copy-start(bf16[32,6,24,336]{3,2,1,0:T(8,128)(2,1)S(1)} %convolution_convert_fusion) | copy-start | bytes 9289732
  14.3 37.2 %collective-permute-start.2 = (bf16[32,2,24,336]{3,2,1,0:T(8,128)(2,1)}, bf16[32,2,24,336]{3,2,1,0:T(8,128)(2,1)S(1)}, u32[]{:S(2)}, u32[]{:S(2)}) collective-permute-start(bf16[32,2,24,336]{3,2,1,0:T(8,128)(2,1)} %get-tuple-element.36), channel_id=1, source_target_pairs={{0,2},{1,3},{4,6},{5,7},{8,10},{9,11},{12,14},{13,15},{16,18},{17,... | collective-permute-start | bytes 3096584 | tf_op jit(solution)/shard_map/ppermute | solution.py:15
  19.2 33.5 %collective-permute-start.3 = (bf16[32,2,24,336]{3,2,1,0:T(8,128)(2,1)}, bf16[32,2,24,336]{3,2,1,0:T(8,128)(2,1)}, u32[]{:S(2)}, u32[]{:S(2)}) collective-permute-start(bf16[32,2,24,336]{3,2,1,0:T(8,128)(2,1)} %get-tuple-element.37), channel_id=1, source_target_pairs={{2,0},{3,1},{6,4},{7,5},{10,8},{11,9},{14,12},{15,13},{18,16},{19,... | collective-permute-start | bytes 3096584 | tf_op jit(solution)/shard_map/ppermute | solution.py:17
  20.7 24.6 %collective-permute-start = (bf16[1,2,24,336]{3,2,1,0:T(8,128)(2,1)S(1)}, bf16[1,2,24,336]{3,2,1,0:T(8,128)(2,1)S(1)}, u32[]{:S(2)}, u32[]{:S(2)}) collective-permute-start(bf16[1,2,24,336]{3,2,1,0:T(8,128)(2,1)S(1)} %get-tuple-element.40), channel_id=1, source_target_pairs={{0,2},{1,3},{4,6},{5,7},{8,10},{9,11},{12,14},{13,15},{16,18},{17,... | collective-permute-start | bytes 96776 | tf_op jit(solution)/shard_map/ppermute | solution.py:15
  26.3 23.2 %collective-permute-start.1 = (bf16[1,2,24,336]{3,2,1,0:T(8,128)(2,1)S(1)}, bf16[1,2,24,336]{3,2,1,0:T(8,128)(2,1)S(1)}, u32[]{:S(2)}, u32[]{:S(2)}) collective-permute-start(bf16[1,2,24,336]{3,2,1,0:T(8,128)(2,1)S(1)} %get-tuple-element.41), channel_id=1, source_target_pairs={{2,0},{3,1},{6,4},{7,5},{10,8},{11,9},{14,12},{15,13},{18,16},{19,... | collective-permute-start | bytes 96776 | tf_op jit(solution)/shard_map/ppermute | solution.py:17
  27.7 23.8 %copy-start.10 = (f32[336]{0:T(512)}, f32[336]{0:T(512)S(1)}, u32[]{:S(2)}) copy-start(f32[336]{0:T(512)S(1)} %get-tuple-element.10) | copy-start | bytes 4036
  27.7 23.8 %copy-start.11 = (f32[336]{0:T(512)}, f32[336]{0:T(512)S(1)}, u32[]{:S(2)}) copy-start(f32[336]{0:T(512)S(1)} %get-tuple-element.11) | copy-start | bytes 4036
  27.7 23.8 %copy-start.12 = (f32[336]{0:T(512)}, f32[336]{0:T(512)S(1)}, u32[]{:S(2)}) copy-start(f32[336]{0:T(512)S(1)} %get-tuple-element.12) | copy-start | bytes 4036
  27.7 23.8 %copy-start.13 = (f32[336]{0:T(512)}, f32[336]{0:T(512)S(1)}, u32[]{:S(2)}) copy-start(f32[336]{0:T(512)S(1)} %get-tuple-element.13) | copy-start | bytes 4036
  27.7 23.8 %copy-start.14 = (f32[336]{0:T(512)}, f32[336]{0:T(512)S(1)}, u32[]{:S(2)}) copy-start(f32[336]{0:T(512)S(1)} %get-tuple-element.14) | copy-start | bytes 4036
  27.7 23.8 %copy-start.15 = (f32[336]{0:T(512)}, f32[336]{0:T(512)S(1)}, u32[]{:S(2)}) copy-start(f32[336]{0:T(512)S(1)} %get-tuple-element.15) | copy-start | bytes 4036
  27.8 23.8 %copy-start.16 = (f32[336]{0:T(512)}, f32[336]{0:T(512)S(1)}, u32[]{:S(2)}) copy-start(f32[336]{0:T(512)S(1)} %get-tuple-element.16) | copy-start | bytes 4036
  27.8 23.8 %copy-start.17 = (f32[336]{0:T(512)}, f32[336]{0:T(512)S(1)}, u32[]{:S(2)}) copy-start(f32[336]{0:T(512)S(1)} %get-tuple-element.17) | copy-start | bytes 4036
  27.8 23.8 %copy-start.18 = (f32[336]{0:T(512)}, f32[336]{0:T(512)S(1)}, u32[]{:S(2)}) copy-start(f32[336]{0:T(512)S(1)} %get-tuple-element.18) | copy-start | bytes 4036
  27.8 23.8 %copy-start.19 = (f32[336]{0:T(512)}, f32[336]{0:T(512)S(1)}, u32[]{:S(2)}) copy-start(f32[336]{0:T(512)S(1)} %get-tuple-element.19) | copy-start | bytes 4036
  27.8 23.8 %copy-start.20 = (f32[336]{0:T(512)}, f32[336]{0:T(512)S(1)}, u32[]{:S(2)}) copy-start(f32[336]{0:T(512)S(1)} %get-tuple-element.20) | copy-start | bytes 4036
  27.8 23.8 %copy-start.21 = (f32[336]{0:T(512)}, f32[336]{0:T(512)S(1)}, u32[]{:S(2)}) copy-start(f32[336]{0:T(512)S(1)} %get-tuple-element.21) | copy-start | bytes 4036
  27.9 23.8 %copy-start.22 = (f32[336]{0:T(512)}, f32[336]{0:T(512)S(1)}, u32[]{:S(2)}) copy-start(f32[336]{0:T(512)S(1)} %get-tuple-element.22) | copy-start | bytes 4036
  27.9 23.8 %copy-start.23 = (f32[336]{0:T(512)}, f32[336]{0:T(512)S(1)}, u32[]{:S(2)}) copy-start(f32[336]{0:T(512)S(1)} %get-tuple-element.23) | copy-start | bytes 4036
  27.9 23.8 %copy-start.24 = (f32[336]{0:T(512)}, f32[336]{0:T(512)S(1)}, u32[]{:S(2)}) copy-start(f32[336]{0:T(512)S(1)} %get-tuple-element.24) | copy-start | bytes 4036
  27.9 23.8 %copy-start.25 = (f32[336]{0:T(512)}, f32[336]{0:T(512)S(1)}, u32[]{:S(2)}) copy-start(f32[336]{0:T(512)S(1)} %get-tuple-element.25) | copy-start | bytes 4036
  27.9 23.8 %copy-start.26 = (f32[336]{0:T(512)}, f32[336]{0:T(512)S(1)}, u32[]{:S(2)}) copy-start(f32[336]{0:T(512)S(1)} %get-tuple-element.26) | copy-start | bytes 4036
  27.9 23.8 %copy-start.27 = (f32[336]{0:T(512)}, f32[336]{0:T(512)S(1)}, u32[]{:S(2)}) copy-start(f32[336]{0:T(512)S(1)} %get-tuple-element.27) | copy-start | bytes 4036
  49.5 8.9 %copy-start.2 = (bf16[32,6,24,336]{3,2,1,0:T(8,128)(2,1)S(1)}, bf16[32,6,24,336]{3,2,1,0:T(8,128)(2,1)}, u32[]{:S(2)}) copy-start(bf16[32,6,24,336]{3,2,1,0:T(8,128)(2,1)} %copy-done.1) | copy-start | bytes 9289732
  51.7 1.0 copy-start.4
  58.4 39.7 %copy-start.6 = (f32[672,28]{0,1:T(8,128)S(1)}, f32[672,28]{0,1:T(8,128)}, u32[]{:S(2)}) copy-start(f32[672,28]{0,1:T(8,128)} %param.16) | copy-start | bytes 225796
  85.9 1.8 %copy-start.3 = (bf16[32,6,24,336]{3,2,1,0:T(8,128)(2,1)}, bf16[32,6,24,336]{3,2,1,0:T(8,128)(2,1)S(1)}, u32[]{:S(2)}) copy-start(bf16[32,6,24,336]{3,2,1,0:T(8,128)(2,1)S(1)} %get-tuple-element.33) | copy-start | bytes 9289732
  85.9 63.9 %copy-start.5 = (f32[6,24,336]{2,1,0:T(8,128)S(1)}, f32[6,24,336]{2,1,0:T(8,128)}, u32[]{:S(2)}) copy-start(f32[6,24,336]{2,1,0:T(8,128)} %get-tuple-element.35) | copy-start | bytes 580612
Sparse Core Ops, SparseCore 0:
  116.8 32.9 all-reduce.5
where the time goes:
time: 159 us; the launch traced here: 158 us
  waiting for transfers between devices  48.4 us (30%)
  other arithmetic  43.2 us (27%)
  blocking collectives  24.1 us (15%)
  between operations  15.2 us (10%)
  starting transfers between devices  13.1 us (8%)
  local copies, waits for them, and re-layouts  8.8 us (6%)
  matrix products  5.47 us (3%)
    psum x1, waiting for transfers between devices, on_device(): lax.psum(local_radius.astype(jnp.bfloat16), 'gen').astype(jnp.float32)  28.1 us
    reduce_sum x1, other arithmetic, on_device(): local_radius = jnp.sum(jnp.abs(dw_gens).astype(jnp.float32), axis=0)  27.4 us
    ppermute x2, waiting for transfers between devices, padded_2(): lax.ppermute(tail, axis, [(i, (i + 1) % count) for i in range(ends)])  16.1 us
    psum x1, blocking collectives, on_device(): gate_radius = lax.psum(local_gate, 'gen')  12 us
    ppermute x2, starting transfers between devices, padded_2(): lax.ppermute(tail, axis, [(i, (i + 1) % count) for i in range(ends)])  10.5 us
    psum x1, blocking collectives, on_device(): pool_center, pool_gens = lax.psum((pool_center, pool_gens), 'row')  7.8 us
    unnamed x67, local copies, waits for them, and re-layouts  6.92 us
    concatenate x1, other arithmetic, padded_2(): jnp.concatenate([lax.ppermute(tail, axis, [(i, (i + 1) % count) for i in...  5.74 us
  transfers between devices with their start and end apart: 5, of which 3 were waited for; matrix products, arithmetic and copies ran while one was open for 5% of the time, Pallas kernels for 0%

commit v1 on v0

--- a/solution.py
+++ b/solution.py
@@ -70,7 +70,9 @@
         jnp.pad(exp_gens, ((0, 0), (0, 0), (margin, margin), (0, 0))), w_depth, row_count, col_count
     ).astype(jnp.bfloat16)
     local_radius = jnp.sum(jnp.abs(dw_gens).astype(jnp.float32), axis=0)
-    feat_radius = lax.psum(local_radius.astype(jnp.bfloat16), "gen").astype(jnp.float32)
+    feat_radius = jnp.sum(lax.all_gather(local_radius.astype(jnp.bfloat16), "gen"), axis=0).astype(
+        jnp.float32
+    )
     inv_cells = 1.0 / (height * col_count)
     pool_center = jnp.sum(dw_center, axis=(0, 1)) * inv_cells
     pool_gens = jnp.sum(dw_gens.astype(jnp.float32), axis=(1, 2)) * inv_cells

time: 159 us -> 133 us (0.84)
  waiting for transfers between devices: 48.4 us -> 20.3 us
  blocking collectives: 24.1 us -> 39.8 us
  between operations: 15.2 us -> 1.9 us
    psum x1 -> x0, waiting for transfers between devices: 28.1 us -> none  [on_device(): lax.psum(local_radius.astype(jnp.bfloat16), 'gen').astype(jnp.float32)]
    all_gather x0 -> x1, blocking collectives: none -> 15.7 us  [on_device(): lax.all_gather(local_radius.astype(jnp.bfloat16), 'gen')]
    unnamed x67 -> x71, local copies, waits for them, and re-layouts: 6.92 us -> 6.97 us
  transfers between devices with their start and end apart: 5 -> 4, of which waited for: 3 -> 2; matrix products, arithmetic and copies ran while one was open for 5% -> 2% of each run, Pallas kernels for 0% -> 0%
where the time goes in v1:
time: 133 us; the launch traced here: 132 us
  other arithmetic  41.9 us (32%)
  blocking collectives  39.8 us (30%)
  waiting for transfers between devices  20.3 us (15%)
  starting transfers between devices  13.1 us (10%)
  local copies, waits for them, and re-layouts  8.84 us (7%)
  matrix products  6.6 us (5%)
  between operations  1.9 us (1%)
    reduce_sum x1, other arithmetic, on_device(): local_radius = jnp.sum(jnp.abs(dw_gens).astype(jnp.float32), axis=0)  27 us
    ppermute x2, waiting for transfers between devices, padded_2(): lax.ppermute(tail, axis, [(i, (i + 1) % count) for i in range(ends)])  16.1 us
    all_gather x1, blocking collectives, on_device(): lax.all_gather(local_radius.astype(jnp.bfloat16), 'gen')  15.7 us
    psum x1, blocking collectives, on_device(): gate_radius = lax.psum(local_gate, 'gen')  12 us
    ppermute x2, starting transfers between devices, padded_2(): lax.ppermute(tail, axis, [(i, (i + 1) % count) for i in range(ends)])  10.5 us
    psum x1, blocking collectives, on_device(): pool_center, pool_gens = lax.psum((pool_center, pool_gens), 'row')  7.78 us
    unnamed x71, local copies, waits for them, and re-layouts  6.97 us
    concatenate x1, other arithmetic, padded_2(): jnp.concatenate([lax.ppermute(tail, axis, [(i, (i + 1) % count) for i in...  5.74 us
  transfers between devices with their start and end apart: 4, of which 2 were waited for; matrix products, arithmetic and copies ran while one was open for 2% of the time, Pallas kernels for 0%

profile of v1, /device:TPU:0, one launch (start us, length us, event | category | flops | bytes accessed | tf_op | source)
XLA Modules:
  0.0 132.4 jit_solution(4649557658557100245)
XLA Ops:
  0.6 0.0 copy-start
  0.6 0.0 copy-start.32
  0.7 0.0 copy-start.6
  0.7 0.0 copy-start.7
  0.7 1.3 copy-done
  2.0 2.3 %convolution_convert_fusion = bf16[32,6,24,336]{3,2,1,0:T(8,128)(2,1)S(1)} fusion(bf16[32,6,24,112]{3,2,1,0:T(8,128)(2,1)S(1)} %copy-done, bf16[112,336]{1,0:T(8,128)(2,1)} %param.12), kind=kOutput, calls=%fused_computation.22 | convolution fusion | flops 348364800 | bytes 4204032 | tf_op jit(solution)/shard_map/dot_general | solution.py:57
  4.3 0.0 copy-start.1
  4.3 1.8 %copy-done.1 = bf16[32,6,24,336]{3,2,1,0:T(8,128)(2,1)} copy-done((bf16[32,6,24,336]{3,2,1,0:T(8,128)(2,1)}, bf16[32,6,24,336]{3,2,1,0:T(8,128)(2,1)S(1)}, u32[]{:S(2)}) %copy-start.1) | copy-done | bytes 3096600
  6.1 1.6 %fusion.48 = (bf16[32,2,24,336]{3,2,1,0:T(8,128)(2,1)}, bf16[32,2,24,336]{3,2,1,0:T(8,128)(2,1)}) fusion(bf16[32,6,24,336]{3,2,1,0:T(8,128)(2,1)S(1)} %convolution_convert_fusion), kind=kLoop, calls=%fused_computation.132 | loop fusion | bytes 4128768 | tf_op jit(solution)/shard_map/slice | solution.py:12
  7.7 4.9 %collective-permute-start.2 = (bf16[32,2,24,336]{3,2,1,0:T(8,128)(2,1)}, bf16[32,2,24,336]{3,2,1,0:T(8,128)(2,1)S(1)}, u32[]{:S(2)}, u32[]{:S(2)}) collective-permute-start(bf16[32,2,24,336]{3,2,1,0:T(8,128)(2,1)} %get-tuple-element.36), channel_id=1, source_target_pairs={{0,2},{1,3},{4,6},{5,7},{8,10},{9,11},{12,14},{13,15},{16,18},{17,... | collective-permute-start | bytes 3096584 | tf_op jit(solution)/shard_map/ppermute | solution.py:15
  12.6 1.3 collective-permute-start.3
  14.0 0.2 fusion.10
  14.2 5.6 %collective-permute-start = (bf16[1,2,24,336]{3,2,1,0:T(8,128)(2,1)S(1)}, bf16[1,2,24,336]{3,2,1,0:T(8,128)(2,1)S(1)}, u32[]{:S(2)}, u32[]{:S(2)}) collective-permute-start(bf16[1,2,24,336]{3,2,1,0:T(8,128)(2,1)S(1)} %get-tuple-element.40), channel_id=1, source_target_pairs={{0,2},{1,3},{4,6},{5,7},{8,10},{9,11},{12,14},{13,15},{16,18},{17,... | collective-permute-start | bytes 96776 | tf_op jit(solution)/shard_map/ppermute | solution.py:15
  19.7 1.3 collective-permute-start.1
  21.1 0.1 slice_reduce_fusion.24
  21.4 0.0 copy-start.28
  21.4 0.0 copy-done.32
  21.4 0.6 dynamic-slice
  22.7 16.1 %collective-permute-done = bf16[1,2,24,336]{3,2,1,0:T(8,128)(2,1)S(1)} collective-permute-done((bf16[1,2,24,336]{3,2,1,0:T(8,128)(2,1)S(1)}, bf16[1,2,24,336]{3,2,1,0:T(8,128)(2,1)S(1)}, u32[]{:S(2)}, u32[]{:S(2)}) %collective-permute-start) | collective-permute-done | bytes 32288 | tf_op jit(solution)/shard_map/ppermute | solution.py:15
  38.8 4.2 %collective-permute-done.1 = bf16[1,2,24,336]{3,2,1,0:T(8,128)(2,1)S(1)} collective-permute-done((bf16[1,2,24,336]{3,2,1,0:T(8,128)(2,1)S(1)}, bf16[1,2,24,336]{3,2,1,0:T(8,128)(2,1)S(1)}, u32[]{:S(2)}, u32[]{:S(2)}) %collective-permute-start.1) | collective-permute-done | bytes 32288 | tf_op jit(solution)/shard_map/ppermute | solution.py:17
  43.0 0.0 copy-start.2
  43.0 1.3 %fusion.46 = (f32[336]{0:T(512)S(1)}, f32[6,24,336]{2,1,0:T(8,128)}) fusion(f32[336]{0:T(512)S(1)} %copy-done.31, f32[336]{0:T(512)S(1)} %get-tuple-element.26, f32[336]{0:T(512)S(1)} %get-tuple-element.27, f32[336]{0:T(512)S(1)} %get-tuple-element.4, bf16[1,2,24,336]{3,2,1,0:T(8,128)(2,1)S(1)} %collective-permute-done.1, ...), kind=kLoop, calls=%fused_computation.131 | loop fusion | flops 4450992 | bytes 649152 | tf_op jit(solution)/shard_map/reduce_sum | solution.py:77
  44.4 0.6 broadcast_multiply_fusion.3
  44.9 0.0 collective-permute-done.2
  45.2 1.0 copy-done.4
  46.2 0.0 collective-permute-done.3
  46.2 5.7 %fusion.5 = bf16[32,10,28,336]{3,2,1,0:T(8,128)(2,1)S(1)} fusion(bf16[32,2,24,336]{3,2,1,0:T(8,128)(2,1)} %collective-permute-done.3, bf16[32,6,24,336]{3,2,1,0:T(8,128)(2,1)} %copy-done.1, bf16[32,2,24,336]{3,2,1,0:T(8,128)(2,1)} %copy-done.4), kind=kLoop, calls=%fused_computation.9 | loop fusion | flops 36126720 | bytes 11182080 | tf_op jit(solution)/shard_map/concatenate | solution.py:13
  51.9 27.0 %abs_reduce_fusion = (bf16[6,24,336]{2,1,0:T(8,128)(2,1)S(1)}, bf16[32,6,24,336]{3,2,1,0:T(8,128)(2,1)S(1)}) fusion(f32[336]{0:T(512)} %copy-done.28, bf16[32,10,28,336]{3,2,1,0:T(8,128)(2,1)S(1)} %fusion.5, f32[336]{0:T(512)} %copy-done.29, f32[336]{0:T(512)S(1)} %get-tuple-element.4, bf16[32,2,24,336]{3,2,1,0:T(8,128)(2,1)} %collective-permute-done.3, ...), kind=kLoop, calls=%fused_computation.21 | loop fusion | flops 125362944 | bytes 70319424 | tf_op jit(solution)/shard_map/reduce_sum | solution.py:72
  78.9 0.0 copy-start.3
  78.9 0.0 copy-start.5
  78.9 1.8 %copy-done.3 = bf16[32,6,24,336]{3,2,1,0:T(8,128)(2,1)} copy-done((bf16[32,6,24,336]{3,2,1,0:T(8,128)(2,1)}, bf16[32,6,24,336]{3,2,1,0:T(8,128)(2,1)S(1)}, u32[]{:S(2)}) %copy-start.3) | copy-done | bytes 3096600
  80.7 0.6 convert_reduce_fusion
  81.3 7.8 %all-reduce.3 = (f32[336]{0:T(512)S(1)}, f32[32,336]{1,0:T(8,128)S(1)}) all-reduce(f32[336]{0:T(512)} %broadcast_multiply_fusion.3, f32[32,336]{1,0:T(8,128)S(1)} %broadcast_multiply_fusion.2), channel_id=1, replica_groups=mesh['grp'=2,'gen'=4,'row'=2,'ch'=2] {'row'}, use_global_device_ids=true, to_apply=%region_1.2 | all-reduce | flops 11088 | bytes 88704 | tf_op jit(solution)/shard_map/psum | solution.py:79
  89.1 1.9 %all-gather.1 = f32[2,336,32]{1,2,0:T(8,128)S(1)} all-gather(f32[1,336,32]{1,2,0:T(8,128)S(1)} %bitcast.64), channel_id=1, replica_groups=mesh['grp'=2,'gen'=4,'row'=2,'ch'=2] {'ch'}, dimensions={0}, use_global_device_ids=true | all-gather | bytes 129024 | tf_op jit(solution)/shard_map/all_gather | solution.py:82
  91.0 0.1 copy.13
  91.1 0.1 reshape.63
  91.2 1.1 fusion.50
  92.3 1.0 abs_reduce_fusion.1
  93.3 12.0 %psum.23 = f32[336]{0:T(512)S(1)} all-reduce(f32[336]{0:T(512)S(1)} %get-tuple-element.45), channel_id=1, replica_groups=mesh['grp'=2,'gen'=4,'row'=2,'ch'=2] {'gen'}, use_global_device_ids=true, to_apply=%region_5.6 | all-reduce | flops 336 | bytes 2688 | tf_op jit(solution)/shard_map/psum | solution.py:89
  105.3 0.2 dynamic-update-slice
  105.5 2.4 %all-reduce.2 = f32[672]{0:T(1024)S(1)} all-reduce(f32[672]{0:T(1024)S(1)} %dynamic-update-slice), channel_id=1, replica_groups=mesh['grp'=2,'gen'=4,'row'=2,'ch'=2] {'ch'}, use_global_device_ids=true, to_apply=%add.2 | all-reduce | flops 672 | bytes 5376
  108.0 1.1 fusion.12
  109.0 1.0 convolution_reduce_fusion
  110.0 0.7 subtract_multiply_fusion.2
  110.8 15.7 %all-gather = bf16[24,24,336]{2,1,0:T(8,128)(2,1)S(1)} all-gather(bf16[6,24,336]{2,1,0:T(8,128)(2,1)S(1)} %get-tuple-element.32), channel_id=2, replica_groups=mesh['grp'=2,'gen'=4,'row'=2,'ch'=2] {'gen'}, dimensions={0}, use_global_device_ids=true | all-gather | bytes 483840 | tf_op jit(solution)/shard_map/all_gather | solution.py:73
  126.5 0.1 reduce_sum.55
  126.5 5.0 %fusion.7 = bf16[32,6,24,336]{3,2,1,0:T(8,128)(2,1)} fusion(bf16[32,6,24,336]{3,2,1,0:T(8,128)(2,1)} %copy-done.3, f32[336]{0:T(512)S(1)} %get-tuple-element.43, f32[32,336]{1,0:T(8,128)S(1)} %broadcast_multiply_fusion.1, f32[6,24,336]{2,1,0:T(8,128)} %get-tuple-element.35), kind=kLoop, calls=%fused_computation.11 | loop fusion | flops 7741440 | bytes 6431040 | tf_op jit(solution)/shard_map/convert_element_type | solution.py:96
  131.5 0.8 multiply_add_fusion
  (60 shorter events, 0.2 us)
Async XLA Ops:
  0.6 1.4 %copy-start = (bf16[32,6,24,112]{3,2,1,0:T(8,128)(2,1)S(1)}, bf16[32,6,24,112]{3,2,1,0:T(8,128)(2,1)}, u32[]{:S(2)}) copy-start(bf16[32,6,24,112]{3,2,1,0:T(8,128)(2,1)} %param.11) | copy-start | bytes 3096580
  0.6 20.8 %copy-start.32 = (u32[32]{0:T(128)S(1)}, u32[32]{0:T(128)}, u32[]{:S(2)}) copy-start(u32[32]{0:T(128)} %constant.21) | copy-start | bytes 388
  0.7 13.3 %copy-start.6 = (bf16[112,336]{1,0:T(8,128)(2,1)S(1)}, bf16[112,336]{1,0:T(8,128)(2,1)}, u32[]{:S(2)}) copy-start(bf16[112,336]{1,0:T(8,128)(2,1)} %param.12) | copy-start | bytes 225796
  0.7 13.3 %copy-start.7 = (bf16[6,24,112]{2,1,0:T(8,128)(2,1)S(1)}, bf16[6,24,112]{2,1,0:T(8,128)(2,1)}, u32[]{:S(2)}) copy-start(bf16[6,24,112]{2,1,0:T(8,128)(2,1)} %param.10) | copy-start | bytes 96772
  0.7 13.3 %copy-start.30 = (f32[336]{0:T(512)S(1)}, f32[336]{0:T(512)}, u32[]{:S(2)}) copy-start(f32[336]{0:T(512)} %param.13) | copy-start | bytes 4036
  0.7 20.4 %copy-start.8 = (f32[5,5,336]{2,1,0:T(8,128)S(1)}, f32[5,5,336]{2,1,0:T(8,128)}, u32[]{:S(2)}) copy-start(f32[5,5,336]{2,1,0:T(8,128)} %param.14) | copy-start | bytes 100804
  0.7 42.3 %copy-start.31 = (f32[336]{0:T(512)S(1)}, f32[336]{0:T(512)}, u32[]{:S(2)}) copy-start(f32[336]{0:T(512)} %param.15) | copy-start | bytes 4036
  4.3 1.8 %copy-start.1 = (bf16[32,6,24,336]{3,2,1,0:T(8,128)(2,1)}, bf16[32,6,24,336]{3,2,1,0:T(8,128)(2,1)S(1)}, u32[]{:S(2)}) copy-start(bf16[32,6,24,336]{3,2,1,0:T(8,128)(2,1)S(1)} %convolution_convert_fusion) | copy-start | bytes 9289732
  7.7 37.2 %collective-permute-start.2 = (bf16[32,2,24,336]{3,2,1,0:T(8,128)(2,1)}, bf16[32,2,24,336]{3,2,1,0:T(8,128)(2,1)S(1)}, u32[]{:S(2)}, u32[]{:S(2)}) collective-permute-start(bf16[32,2,24,336]{3,2,1,0:T(8,128)(2,1)} %get-tuple-element.36), channel_id=1, source_target_pairs={{0,2},{1,3},{4,6},{5,7},{8,10},{9,11},{12,14},{13,15},{16,18},{17,... | collective-permute-start | bytes 3096584 | tf_op jit(solution)/shard_map/ppermute | solution.py:15
  12.6 33.5 %collective-permute-start.3 = (bf16[32,2,24,336]{3,2,1,0:T(8,128)(2,1)}, bf16[32,2,24,336]{3,2,1,0:T(8,128)(2,1)}, u32[]{:S(2)}, u32[]{:S(2)}) collective-permute-start(bf16[32,2,24,336]{3,2,1,0:T(8,128)(2,1)} %get-tuple-element.37), channel_id=1, source_target_pairs={{2,0},{3,1},{6,4},{7,5},{10,8},{11,9},{14,12},{15,13},{18,16},{19,... | collective-permute-start | bytes 3096584 | tf_op jit(solution)/shard_map/ppermute | solution.py:17
  14.2 24.6 %collective-permute-start = (bf16[1,2,24,336]{3,2,1,0:T(8,128)(2,1)S(1)}, bf16[1,2,24,336]{3,2,1,0:T(8,128)(2,1)S(1)}, u32[]{:S(2)}, u32[]{:S(2)}) collective-permute-start(bf16[1,2,24,336]{3,2,1,0:T(8,128)(2,1)S(1)} %get-tuple-element.40), channel_id=1, source_target_pairs={{0,2},{1,3},{4,6},{5,7},{8,10},{9,11},{12,14},{13,15},{16,18},{17,... | collective-permute-start | bytes 96776 | tf_op jit(solution)/shard_map/ppermute | solution.py:15
  19.7 23.2 %collective-permute-start.1 = (bf16[1,2,24,336]{3,2,1,0:T(8,128)(2,1)S(1)}, bf16[1,2,24,336]{3,2,1,0:T(8,128)(2,1)S(1)}, u32[]{:S(2)}, u32[]{:S(2)}) collective-permute-start(bf16[1,2,24,336]{3,2,1,0:T(8,128)(2,1)S(1)} %get-tuple-element.41), channel_id=1, source_target_pairs={{2,0},{3,1},{6,4},{7,5},{10,8},{11,9},{14,12},{15,13},{18,16},{19,... | collective-permute-start | bytes 96776 | tf_op jit(solution)/shard_map/ppermute | solution.py:17
  21.2 23.8 %copy-start.9 = (f32[336]{0:T(512)}, f32[336]{0:T(512)S(1)}, u32[]{:S(2)}) copy-start(f32[336]{0:T(512)S(1)} %get-tuple-element.7) | copy-start | bytes 4036
  21.2 23.8 %copy-start.10 = (f32[336]{0:T(512)}, f32[336]{0:T(512)S(1)}, u32[]{:S(2)}) copy-start(f32[336]{0:T(512)S(1)} %get-tuple-element.8) | copy-start | bytes 4036
  21.2 23.8 %copy-start.11 = (f32[336]{0:T(512)}, f32[336]{0:T(512)S(1)}, u32[]{:S(2)}) copy-start(f32[336]{0:T(512)S(1)} %get-tuple-element.9) | copy-start | bytes 4036
  21.2 23.8 %copy-start.12 = (f32[336]{0:T(512)}, f32[336]{0:T(512)S(1)}, u32[]{:S(2)}) copy-start(f32[336]{0:T(512)S(1)} %get-tuple-element.10) | copy-start | bytes 4036
  21.2 23.8 %copy-start.13 = (f32[336]{0:T(512)}, f32[336]{0:T(512)S(1)}, u32[]{:S(2)}) copy-start(f32[336]{0:T(512)S(1)} %get-tuple-element.11) | copy-start | bytes 4036
  21.2 23.8 %copy-start.14 = (f32[336]{0:T(512)}, f32[336]{0:T(512)S(1)}, u32[]{:S(2)}) copy-start(f32[336]{0:T(512)S(1)} %get-tuple-element.12) | copy-start | bytes 4036
  21.2 23.8 %copy-start.15 = (f32[336]{0:T(512)}, f32[336]{0:T(512)S(1)}, u32[]{:S(2)}) copy-start(f32[336]{0:T(512)S(1)} %get-tuple-element.13) | copy-start | bytes 4036
  21.2 23.8 %copy-start.16 = (f32[336]{0:T(512)}, f32[336]{0:T(512)S(1)}, u32[]{:S(2)}) copy-start(f32[336]{0:T(512)S(1)} %get-tuple-element.14) | copy-start | bytes 4036
  21.2 23.8 %copy-start.17 = (f32[336]{0:T(512)}, f32[336]{0:T(512)S(1)}, u32[]{:S(2)}) copy-start(f32[336]{0:T(512)S(1)} %get-tuple-element.15) | copy-start | bytes 4036
  21.2 23.8 %copy-start.18 = (f32[336]{0:T(512)}, f32[336]{0:T(512)S(1)}, u32[]{:S(2)}) copy-start(f32[336]{0:T(512)S(1)} %get-tuple-element.16) | copy-start | bytes 4036
  21.3 23.8 %copy-start.19 = (f32[336]{0:T(512)}, f32[336]{0:T(512)S(1)}, u32[]{:S(2)}) copy-start(f32[336]{0:T(512)S(1)} %get-tuple-element.17) | copy-start | bytes 4036
  21.3 23.8 %copy-start.20 = (f32[336]{0:T(512)}, f32[336]{0:T(512)S(1)}, u32[]{:S(2)}) copy-start(f32[336]{0:T(512)S(1)} %get-tuple-element.18) | copy-start | bytes 4036
  21.3 23.8 %copy-start.21 = (f32[336]{0:T(512)}, f32[336]{0:T(512)S(1)}, u32[]{:S(2)}) copy-start(f32[336]{0:T(512)S(1)} %get-tuple-element.19) | copy-start | bytes 4036
  21.3 23.8 %copy-start.22 = (f32[336]{0:T(512)}, f32[336]{0:T(512)S(1)}, u32[]{:S(2)}) copy-start(f32[336]{0:T(512)S(1)} %get-tuple-element.20) | copy-start | bytes 4036
  21.3 23.8 %copy-start.23 = (f32[336]{0:T(512)}, f32[336]{0:T(512)S(1)}, u32[]{:S(2)}) copy-start(f32[336]{0:T(512)S(1)} %get-tuple-element.21) | copy-start | bytes 4036
  21.4 23.7 %copy-start.24 = (f32[336]{0:T(512)}, f32[336]{0:T(512)S(1)}, u32[]{:S(2)}) copy-start(f32[336]{0:T(512)S(1)} %get-tuple-element.22) | copy-start | bytes 4036
  21.4 23.7 %copy-start.25 = (f32[336]{0:T(512)}, f32[336]{0:T(512)S(1)}, u32[]{:S(2)}) copy-start(f32[336]{0:T(512)S(1)} %get-tuple-element.23) | copy-start | bytes 4036
  21.4 23.7 %copy-start.26 = (f32[336]{0:T(512)}, f32[336]{0:T(512)S(1)}, u32[]{:S(2)}) copy-start(f32[336]{0:T(512)S(1)} %get-tuple-element.24) | copy-start | bytes 4036
  21.4 23.7 %copy-start.27 = (f32[336]{0:T(512)}, f32[336]{0:T(512)S(1)}, u32[]{:S(2)}) copy-start(f32[336]{0:T(512)S(1)} %get-tuple-element.25) | copy-start | bytes 4036
  21.4 23.7 %copy-start.28 = (f32[336]{0:T(512)}, f32[336]{0:T(512)S(1)}, u32[]{:S(2)}) copy-start(f32[336]{0:T(512)S(1)} %get-tuple-element.26) | copy-start | bytes 4036
  21.4 23.7 %copy-start.29 = (f32[336]{0:T(512)}, f32[336]{0:T(512)S(1)}, u32[]{:S(2)}) copy-start(f32[336]{0:T(512)S(1)} %get-tuple-element.27) | copy-start | bytes 4036
  43.0 8.9 %copy-start.2 = (bf16[32,6,24,336]{3,2,1,0:T(8,128)(2,1)S(1)}, bf16[32,6,24,336]{3,2,1,0:T(8,128)(2,1)}, u32[]{:S(2)}) copy-start(bf16[32,6,24,336]{3,2,1,0:T(8,128)(2,1)} %copy-done.1) | copy-start | bytes 9289732
  45.1 1.0 copy-start.4
  78.9 1.8 %copy-start.3 = (bf16[32,6,24,336]{3,2,1,0:T(8,128)(2,1)}, bf16[32,6,24,336]{3,2,1,0:T(8,128)(2,1)S(1)}, u32[]{:S(2)}) copy-start(bf16[32,6,24,336]{3,2,1,0:T(8,128)(2,1)S(1)} %get-tuple-element.33) | copy-start | bytes 9289732
  78.9 52.6 %copy-start.5 = (f32[6,24,336]{2,1,0:T(8,128)S(1)}, f32[6,24,336]{2,1,0:T(8,128)}, u32[]{:S(2)}) copy-start(f32[6,24,336]{2,1,0:T(8,128)} %get-tuple-element.35) | copy-start | bytes 580612
